TPU v7x, 32 devices: a whole 2x2x4 slice. The times are simulated.
32 devices in a mesh: expert: 8 (over y, x, core), tensor: 4 (over z).
Axes of the slice: x: 2, y: 2, z: 4, core: 2. Of those that a mesh axis runs over, the one named last changes fastest.
Arguments:
- inputs: float32 [7880, 512], P('expert'), may hold values from -6 to 6
- cotangent: float32 [7880, 512], P('expert'), may hold values from -6 to 6
- routes: int32 [2, 7880, 2], P(None, 'expert'), may hold values from 0 to 7, all different within a row
- priority: int32 [2, 7880], P(None, 'expert'), may hold values from 0 to 984, as said below
- attend_in: float32 [2, 3, 512, 512], P(None, None, 'expert', 'tensor'), may hold values from -0.375 to 0.375
- attend_out: float32 [2, 512, 512], P(None, 'tensor', 'expert'), may hold values from -1.5 to 1.5
- router: float32 [2, 512, 8], P(None, None, 'expert'), may hold values from -0.1875 to 0.1875
- norm_gains: float32 [2, 2, 512], P(None, None, 'expert'), may hold values from 0.25 to 1.75
- expert_in: float32 [2, 8, 512, 2048], P(None, 'expert', None, 'tensor'), may hold values from -0.25 to 0.25
- expert_out: float32 [2, 8, 2048, 512], P(None, 'expert', 'tensor'), may hold values from -0.5 to 0.5
Outputs:
- outputs: float32 [7880, 512], P('expert')
- input_grad: float32 [7880, 512], P('expert')
- attend_in_grad: float32 [2, 3, 512, 512], P(None, None, 'expert', 'tensor')
- attend_out_grad: float32 [2, 512, 512], P(None, 'tensor', 'expert')
- router_grad: float32 [2, 512, 8], P(None, None, 'expert')
- gains_grad: float32 [2, 2, 512], P(None, None, 'expert')
- expert_in_grad: float32 [2, 8, 512, 2048], P(None, 'expert', None, 'tensor')
- expert_out_grad: float32 [2, 8, 2048, 512], P(None, 'expert', 'tensor')
Inputs may be any that keep to these rules, and one draw needn't show every extreme that they name: `routes`: in each block each token names two different experts, and every expert is named by some token. `priority`: in each block, the values within each device's 985 tokens are a permutation.
All inputs are finite; a program needn't handle non-finite values.
Results may differ from a plain program's by a relative error of at most 0.025.
The roundings to bfloat16 on the way count: a program that leaves them out, or rounds other values in their place, can miss the bound.
Values may be sent and summed in bfloat16 or wider, within the bound.
A program may use at most 192 MiB of HBM per device.

v0:
```python
import jax
import jax.numpy as jnp
from jax import lax
from jax.sharding import PartitionSpec as P

HEAD_DIM = 64
SEQ = 197


def norm_rows(rows_in, gain_row):
    centred = rows_in - jnp.mean(rows_in, axis=-1, keepdims=True)
    spread = jnp.mean(centred * centred, axis=-1, keepdims=True)
    return centred * lax.rsqrt(spread + 1e-06) * gain_row


def gelu_exact(rows_in):
    return 0.5 * rows_in * (1.0 + lax.erf(rows_in * 0.7071067811865476))


def contract_rows(left_side, right_side):
    return lax.dot_general(
        left_side, right_side, (((0,), (0,)), ((), ())), preferred_element_type=jnp.float32
    )


def contract_last(left_side, right_side):
    return lax.dot_general(
        left_side, right_side, (((1,), (1,)), ((), ())), preferred_element_type=jnp.float32
    )


def heads_total(partial_sum):
    return lax.psum(partial_sum, "tensor")


def to_experts(make_rows, model_width):
    return lax.all_to_all(
        make_rows(0, model_width), "expert", split_axis=0, concat_axis=0, tiled=True
    )


def to_sources(partial_rows):
    shares = lax.psum_scatter(partial_rows, "tensor", scatter_dimension=2, tiled=True)
    moved = lax.all_to_all(
        shares.astype(jnp.bfloat16), "expert", split_axis=0, concat_axis=0, tiled=True
    )
    return lax.all_gather(moved, "tensor", axis=2, tiled=True)


def slot_plan(chosen, rank_rows, experts, capacity):
    columns = lax.broadcasted_iota(jnp.int32, (1, experts), 1)
    first_hot = (chosen[:, 0:1] == columns).astype(jnp.bfloat16)
    second = (chosen[:, 1:2] == columns).astype(jnp.bfloat16)
    earlier = (rank_rows[None, :] < rank_rows[:, None]).astype(jnp.bfloat16)
    count_first = jnp.dot(earlier, first_hot, preferred_element_type=jnp.float32)
    count_second = jnp.dot(earlier, second, preferred_element_type=jnp.float32)
    first_f = first_hot.astype(jnp.float32)
    second_f = second.astype(jnp.float32)
    filled = jnp.sum(first_f, axis=0, keepdims=True)
    slot_first = jnp.sum(count_first * first_f, axis=1)
    slot_second = jnp.sum((filled + count_second) * second_f, axis=1)
    slot_nums = jnp.stack([slot_first, slot_second], axis=1).astype(jnp.int32)
    target = jnp.where(slot_nums < capacity, chosen * capacity + slot_nums, experts * capacity)
    return (target, first_f, second_f)


def local(
    inputs,
    cotangent,
    routes,
    priority,
    attend_in,
    attend_out,
    router,
    norm_gains,
    expert_in,
    expert_out,
):
    experts = lax.axis_size("expert")
    tokens = inputs.shape[0]
    model_width = inputs.shape[1]
    images = tokens // SEQ
    local_heads = attend_in.shape[3] // HEAD_DIM
    layers = attend_in.shape[0]
    capacity = max(2, (10 * tokens + 4 * experts - 1) // (4 * experts))
    slots_all = experts * capacity
    score_scale = HEAD_DIM ** (-0.5)
    in_full, out_full, router_full, gains_full = (
        lax.all_gather(attend_in.astype(jnp.bfloat16), "expert", axis=2, tiled=True),
        lax.all_gather(attend_out.astype(jnp.bfloat16), "expert", axis=2, tiled=True),
        lax.all_gather(router.astype(jnp.bfloat16), "expert", axis=2, tiled=True),
        lax.all_gather(norm_gains.astype(jnp.bfloat16), "expert", axis=2, tiled=True),
    )
    slot_ids = lax.broadcasted_iota(jnp.int32, (1, slots_all), 1)
    stream = inputs
    stash_list = []
    for layer_index in range(layers):
        gains_now = gains_full[layer_index].astype(jnp.float32)
        normed = norm_rows(stream, gains_now[0]).astype(jnp.bfloat16)
        project = in_full[layer_index]
        triple = jnp.einsum(
            "td,jdh->jth", normed, project, preferred_element_type=jnp.float32
        ).astype(jnp.bfloat16)
        shaped = triple.reshape(3, images, SEQ, local_heads, HEAD_DIM)
        scores = (
            jnp.einsum("iqhd,ikhd->ihqk", shaped[0], shaped[1], preferred_element_type=jnp.float32)
            * score_scale
        )
        log_total = jax.nn.logsumexp(scores, axis=-1, keepdims=True)
        attention = jnp.exp(scores - log_total).astype(jnp.bfloat16)
        mixed_heads = (
            jnp.einsum("ihqk,ikhd->iqhd", attention, shaped[2], preferred_element_type=jnp.float32)
            .astype(jnp.bfloat16)
            .reshape(tokens, -1)
        )
        middle = stream + heads_total(
            jnp.dot(mixed_heads, out_full[layer_index], preferred_element_type=jnp.float32)
        )
        normed_two = norm_rows(middle, gains_now[1]).astype(jnp.bfloat16)
        logits = jnp.dot(normed_two, router_full[layer_index], preferred_element_type=jnp.float32)
        probs_all = jax.nn.softmax(logits, axis=-1)
        chosen = routes[layer_index]
        gate_values = jnp.take_along_axis(probs_all, chosen, axis=1)
        target, first_f, second_f = slot_plan(chosen, priority[layer_index], experts, capacity)
        pick_first = (target[:, 0:1] == slot_ids).astype(jnp.bfloat16)
        pick_second = (target[:, 1:2] == slot_ids).astype(jnp.bfloat16)
        pick_both = pick_first + pick_second

        def dispatch_rows(first_col, col_count, normed_two=normed_two, pick_both=pick_both):
            return (
                contract_rows(pick_both, normed_two)
                .astype(jnp.bfloat16)
                .reshape(experts, capacity, col_count)
            )

        arrived = to_experts(dispatch_rows, model_width).reshape(slots_all, model_width)
        win_now = expert_in[layer_index, 0].astype(jnp.bfloat16)
        wout_now = expert_out[layer_index, 0].astype(jnp.bfloat16)
        before = jnp.dot(arrived, win_now, preferred_element_type=jnp.float32)
        hidden = gelu_exact(before).astype(jnp.bfloat16)
        expert_rows = jnp.dot(hidden, wout_now, preferred_element_type=jnp.float32).reshape(
            experts, capacity, model_width
        )
        returned = to_sources(expert_rows).reshape(slots_all, model_width)
        rows_first = jnp.dot(pick_first, returned, preferred_element_type=jnp.float32)
        rows_second = jnp.dot(pick_second, returned, preferred_element_type=jnp.float32)
        output = middle + gate_values[:, 0:1] * rows_first + gate_values[:, 1:2] * rows_second
        kept_pre = None
        stash_list.append(
            (
                stream,
                gains_now,
                normed,
                shaped,
                log_total,
                mixed_heads,
                middle,
                normed_two,
                probs_all,
                gate_values,
                target,
                first_f,
                second_f,
                pick_first,
                pick_second,
                pick_both,
                arrived,
                rows_first,
                rows_second,
                kept_pre,
            )
        )
        stream = output
    upstream = cotangent
    grads_in, grads_out, grads_router, grads_gain, grads_win, grads_wout = ([], [], [], [], [], [])
    for layer_index in reversed(range(layers)):
        (
            stream_in,
            gains_now,
            normed,
            shaped,
            log_total,
            mixed_heads,
            middle,
            normed_two,
            probs_all,
            gate_values,
            target,
            first_f,
            second_f,
            pick_first,
            pick_second,
            pick_both,
            arrived,
            rows_first,
            rows_second,
            kept_pre,
        ) = stash_list[layer_index]
        win_now = expert_in[layer_index, 0].astype(jnp.bfloat16)
        wout_now = expert_out[layer_index, 0].astype(jnp.bfloat16)
        gate_first = jnp.sum(upstream * rows_first, axis=1)
        gate_second = jnp.sum(upstream * rows_second, axis=1)
        scaled = jnp.concatenate(
            [
                gate_values[:, 0:1] * upstream,
                gate_values[:, 1:2] * upstream,
                jnp.zeros((1, model_width), jnp.float32),
            ],
            axis=0,
        )
        owners = (
            jnp.full((slots_all + 1,), 2 * tokens, jnp.int32)
            .at[jnp.concatenate([target[:, 0], target[:, 1]])]
            .set(jnp.arange(2 * tokens, dtype=jnp.int32))[:slots_all]
        )

        def gradient_rows(first_col, col_count, scaled=scaled, owners=owners):
            return (
                jnp.take(scaled, owners, axis=0)
                .astype(jnp.bfloat16)
                .reshape(experts, capacity, col_count)
            )

        grad_arrived = to_experts(gradient_rows, model_width).reshape(slots_all, model_width)
        before = jnp.dot(arrived, win_now, preferred_element_type=jnp.float32)
        hidden = gelu_exact(before).astype(jnp.bfloat16)
        grads_wout.append(contract_rows(hidden, grad_arrived))
        grad_hidden = contract_last(grad_arrived, wout_now)
        grad_before = jax.vjp(gelu_exact, before)[1](grad_hidden)[0].astype(jnp.bfloat16)
        grads_win.append(contract_rows(arrived, grad_before))
        grad_rows = contract_last(grad_before, win_now).reshape(experts, capacity, model_width)
        grad_dispatched = to_sources(grad_rows).reshape(slots_all, model_width)
        grad_normed = jnp.dot(pick_both, grad_dispatched, preferred_element_type=jnp.float32)
        grad_probs = first_f * gate_first[:, None] + second_f * gate_second[:, None]
        grad_logits = (
            probs_all * (grad_probs - jnp.sum(probs_all * grad_probs, axis=1, keepdims=True))
        ).astype(jnp.bfloat16)
        grads_router.append(contract_rows(normed_two, grad_logits))
        grad_normed = grad_normed + contract_last(grad_logits, router_full[layer_index])
        norm_back = jax.vjp(norm_rows, middle, gains_now[1])[1](grad_normed)
        grad_middle = upstream + norm_back[0]
        grad_branch = grad_middle.astype(jnp.bfloat16)
        grads_out.append(contract_rows(mixed_heads, grad_branch))
        grad_mixed = (
            contract_last(grad_branch, out_full[layer_index])
            .astype(jnp.bfloat16)
            .reshape(images, SEQ, local_heads, HEAD_DIM)
        )
        scores = (
            jnp.einsum("iqhd,ikhd->ihqk", shaped[0], shaped[1], preferred_element_type=jnp.float32)
            * score_scale
        )
        attention_f = jnp.exp(scores - log_total)
        attention = attention_f.astype(jnp.bfloat16)
        grad_value = jnp.einsum(
            "ihqk,iqhd->ikhd", attention, grad_mixed, preferred_element_type=jnp.float32
        ).astype(jnp.bfloat16)
        grad_attention = jnp.einsum(
            "iqhd,ikhd->ihqk", grad_mixed, shaped[2], preferred_element_type=jnp.float32
        )
        grad_scores = (
            attention_f
            * (grad_attention - jnp.sum(attention_f * grad_attention, axis=-1, keepdims=True))
        ).astype(jnp.bfloat16)
        grad_query = (
            jnp.einsum(
                "ihqk,ikhd->iqhd", grad_scores, shaped[1], preferred_element_type=jnp.float32
            )
            * score_scale
        ).astype(jnp.bfloat16)
        grad_key = (
            jnp.einsum(
                "ihqk,iqhd->ikhd", grad_scores, shaped[0], preferred_element_type=jnp.float32
            )
            * score_scale
        ).astype(jnp.bfloat16)
        grad_triple = jnp.stack([grad_query, grad_key, grad_value]).reshape(3, tokens, -1)
        grads_in.append(
            jnp.einsum("td,jth->jdh", normed, grad_triple, preferred_element_type=jnp.float32)
        )
        project = in_full[layer_index]
        grad_normed_one = heads_total(
            jnp.einsum("jth,jdh->td", grad_triple, project, preferred_element_type=jnp.float32)
        )
        norm_back_one = jax.vjp(norm_rows, stream_in, gains_now[0])[1](grad_normed_one)
        grads_gain.append(jnp.stack([norm_back_one[1], norm_back[1]]))
        upstream = grad_middle + norm_back_one[0]
    in_grad_all = jnp.stack(grads_in[::-1])
    out_grad_all = jnp.stack(grads_out[::-1])
    router_grad_all = jnp.stack(grads_router[::-1])
    gain_grad_all = jnp.stack(grads_gain[::-1])
    reduced = (
        lax.psum_scatter(in_grad_all, "expert", scatter_dimension=2, tiled=True),
        lax.psum_scatter(out_grad_all, "expert", scatter_dimension=2, tiled=True),
        lax.psum_scatter(router_grad_all, "expert", scatter_dimension=2, tiled=True),
        lax.psum_scatter(gain_grad_all, "expert", scatter_dimension=2, tiled=True),
    )
    win_grad_all = jnp.stack(grads_win[::-1])[:, None]
    wout_grad_all = jnp.stack(grads_wout[::-1])[:, None]
    return (
        stream,
        upstream,
        reduced[0],
        reduced[1],
        reduced[2],
        reduced[3],
        win_grad_all,
        wout_grad_all,
    )


def solution(mesh):
    placed = (
        P("expert", None),
        P("expert", None),
        P(None, "expert", None),
        P(None, "expert"),
        P(None, None, "expert", "tensor"),
        P(None, "tensor", "expert"),
        P(None, None, "expert"),
        P(None, None, "expert"),
        P(None, "expert", None, "tensor"),
        P(None, "expert", "tensor", None),
    )
    return jax.shard_map(
        local,
        mesh=mesh,
        in_specs=placed,
        out_specs=(
            P("expert", None),
            P("expert", None),
            P(None, None, "expert", "tensor"),
            P(None, "tensor", "expert"),
            P(None, None, "expert"),
            P(None, None, "expert"),
            P(None, "expert", None, "tensor"),
            P(None, "expert", "tensor", None),
        ),
        check_vma=False,
    )
```

profile of v0, /device:TPU:0, one launch (start us, length us, event | category | flops | bytes accessed | tf_op | source)
XLA Modules:
  0.0 1557.0 jit_solution(12436539425469895753)
XLA Ops:
  10.5 10.8 all_gather.26
  21.3 9.3 all_gather.24
  30.9 9.4 all_gather.25
  40.4 6.5 slice_reduce_fusion.8
  68.5 78.9 %all-reduce.10.cloned.1.call-done = f32[985,512]{1,0:T(8,128)} async-done(((f32[985,512]{1,0:T(8,128)}), f32[985,512]{1,0:T(8,128)}) %all-reduce.10.cloned.1.call-update) | async-done | bytes 2017296 | tf_op jit(solution)/shard_map/psum | solution.py:33
  151.9 4.0 fusion.41
  158.1 4.8 all-to-all-start
  166.4 28.0 %all-to-all-done = bf16[8,308,512]{2,1,0:T(8,128)(2,1)} async-done(((bf16[8,308,512]{2,1,0:T(8,128)(2,1)}), bf16[8,308,512]{2,1,0:T(8,128)(2,1)}, u32[]{:S(2)}, u32[]{:S(2)}) %all-to-all-start) | async-done | bytes 2523168 | tf_op jit(solution)/shard_map/all_to_all | solution.py:37
  194.5 4.1 reshape.431
  198.6 5.7 multiply_convert_fusion.1
  207.0 4.8 fusion.106
  211.9 89.2 %reduce-scatter.8.cloned.1.call-done = f32[8,308,128]{2,1,0:T(8,128)} async-done(((f32[8,308,512]{2,1,0:T(8,128)}), f32[8,308,128]{2,1,0:T(8,128)}) %reduce-scatter.8.cloned.1.call-update) | async-done | bytes 1261584 | tf_op jit(solution)/shard_map/reduce_scatter | solution.py:43
  302.5 14.6 all_to_all.40
  317.6 8.0 all_gather.27
  327.9 18.5 %gather_fusion = f32[1970]{0:T(1024)S(1)} fusion(f32[985,8]{0,1:T(8,128)S(1)} %fusion.144, s32[1970]{0:T(1024)S(1)} %reshape.507), kind=kCustom, calls=%fused_computation.clone | custom fusion | bytes 31520 | tf_op jit(solution)/shard_map/jit(take_along_axis)/gather | solution.py:123
  347.5 22.3 %all-gather.5.cloned.1.call-done = bf16[8,308,512]{2,1,0:T(8,128)(2,1)} async-done(((bf16[8,308,128]{2,1,0:T(8,128)(2,1)}), bf16[8,308,512]{2,1,0:T(8,128)(2,1)}) %all-gather.5.cloned.1.call-update) | async-done | bytes 2523152 | tf_op jit(solution)/shard_map/all_gather | solution.py:47
  375.4 6.7 fusion.176
  402.9 78.0 %all-reduce.12.cloned.1.call-done = f32[985,512]{1,0:T(8,128)} async-done(((f32[985,512]{1,0:T(8,128)}), f32[985,512]{1,0:T(8,128)}) %all-reduce.12.cloned.1.call-update) | async-done | bytes 2017296 | tf_op jit(solution)/shard_map/psum | solution.py:33
  485.3 5.5 fusion.38
  493.5 35.3 %all_to_all.41 = bf16[8,308,512]{2,1,0:T(8,128)(2,1)} all-to-all(bf16[8,308,512]{2,1,0:T(8,128)(2,1)S(1)} %reshape.434), channel_id=1, replica_groups=mesh['expert'=8,'tensor'=4] {'expert'}, dimensions={0} | all-to-all | bytes 5046272 | tf_op jit(solution)/shard_map/all_to_all | solution.py:37
  528.8 4.2 reshape.435
  533.1 5.6 multiply_convert_fusion
  541.3 4.8 fusion.104
  546.2 89.0 %reduce-scatter.10.cloned.1.call-done = f32[8,308,128]{2,1,0:T(8,128)} async-done(((f32[8,308,512]{2,1,0:T(8,128)}), f32[8,308,128]{2,1,0:T(8,128)}) %reduce-scatter.10.cloned.1.call-update) | async-done | bytes 1261584 | tf_op jit(solution)/shard_map/reduce_scatter | solution.py:43
  636.6 14.6 all_to_all.42
  653.7 10.0 scatter_custom_fusion.1
  663.7 10.0 scatter_custom_fusion
  676.1 27.8 %all-gather.7.cloned.1.call-done = bf16[8,308,512]{2,1,0:T(8,128)(2,1)} async-done(((bf16[8,308,128]{2,1,0:T(8,128)(2,1)}), bf16[8,308,512]{2,1,0:T(8,128)(2,1)}) %all-gather.7.cloned.1.call-update) | async-done | bytes 2523152 | tf_op jit(solution)/shard_map/all_gather | solution.py:47
  703.8 4.5 reshape.436
  708.4 4.7 fusion
  713.1 4.3 multiply_reduce_fusion.13
  718.1 18.5 %gather_fusion.1 = f32[1970]{0:T(1024)S(1)} fusion(f32[985,8]{0,1:T(8,128)S(1)} %get-tuple-element.98, s32[1970]{0:T(1024)S(1)} %reshape.512), kind=kCustom, calls=%fused_computation.2.clone | custom fusion | bytes 31520 | tf_op jit(solution)/shard_map/jit(take_along_axis)/gather | solution.py:123
  739.3 9.0 concatenate.52
  748.3 8.2 gather_fusion.2
  756.5 3.6 select_convert_fusion.1
  762.8 35.0 %all_to_all.43 = bf16[8,308,512]{2,1,0:T(8,128)(2,1)} all-to-all(bf16[8,308,512]{2,1,0:T(8,128)(2,1)S(1)} %reshape.437), channel_id=1, replica_groups=mesh['expert'=8,'tensor'=4] {'expert'}, dimensions={0} | all-to-all | bytes 5046272 | tf_op jit(solution)/shard_map/all_to_all | solution.py:37
  797.9 4.2 reshape.438
  802.1 6.4 add_convert_fusion.1
  811.2 4.9 fusion.102
  816.2 89.2 %reduce-scatter.12.cloned.1.call-done = f32[8,308,128]{2,1,0:T(8,128)} async-done(((f32[8,308,512]{2,1,0:T(8,128)}), f32[8,308,128]{2,1,0:T(8,128)}) %reduce-scatter.12.cloned.1.call-update) | async-done | bytes 1261584 | tf_op jit(solution)/shard_map/reduce_scatter | solution.py:43
  906.8 14.5 all_to_all.44
  921.5 52.5 %all-gather.9.cloned.1.call-done = bf16[8,308,512]{2,1,0:T(8,128)(2,1)} async-done(((bf16[8,308,128]{2,1,0:T(8,128)(2,1)}), bf16[8,308,512]{2,1,0:T(8,128)(2,1)}) %all-gather.9.cloned.1.call-update) | async-done | bytes 2523152 | tf_op jit(solution)/shard_map/all_gather | solution.py:47
  976.8 2.8 fusion.22
  999.3 82.0 %all-reduce.14.cloned.1.call-done = f32[985,512]{1,0:T(8,128)} async-done(((f32[985,512]{1,0:T(8,128)}), f32[985,512]{1,0:T(8,128)}) %all-reduce.14.cloned.1.call-update) | async-done | bytes 2017296 | tf_op jit(solution)/shard_map/psum | solution.py:33
  1088.9 8.7 concatenate.54
  1097.6 8.2 gather_fusion.3
  1105.8 3.7 select_convert_fusion
  1112.2 35.0 %all_to_all.45 = bf16[8,308,512]{2,1,0:T(8,128)(2,1)} all-to-all(bf16[8,308,512]{2,1,0:T(8,128)(2,1)S(1)} %reshape.441), channel_id=1, replica_groups=mesh['expert'=8,'tensor'=4] {'expert'}, dimensions={0} | all-to-all | bytes 5046272 | tf_op jit(solution)/shard_map/all_to_all | solution.py:37
  1147.2 4.3 reshape.442
  1151.5 6.5 add_convert_fusion
  1160.6 4.9 fusion.100
  1165.6 89.0 %reduce-scatter.14.cloned.1.call-done = f32[8,308,128]{2,1,0:T(8,128)} async-done(((f32[8,308,512]{2,1,0:T(8,128)}), f32[8,308,128]{2,1,0:T(8,128)}) %reduce-scatter.14.cloned.1.call-update) | async-done | bytes 1261584 | tf_op jit(solution)/shard_map/reduce_scatter | solution.py:43
  1255.9 14.5 all_to_all.46
  1275.6 47.4 %all-gather.11.cloned.1.call-done = bf16[8,308,512]{2,1,0:T(8,128)(2,1)} async-done(((bf16[8,308,128]{2,1,0:T(8,128)(2,1)}), bf16[8,308,512]{2,1,0:T(8,128)(2,1)}) %all-gather.11.cloned.1.call-update) | async-done | bytes 2523152 | tf_op jit(solution)/shard_map/all_gather | solution.py:47
  1323.1 4.5 reshape.443
  1327.6 4.7 fusion.17
  1360.2 3.8 copy.354
  1364.2 5.2 convolution_bitcast_fusion.2
  1374.4 24.3 %all-reduce.2 = f32[2,512,8]{1,0,2:T(2,128)S(1)} all-reduce(f32[2,512,8]{1,0,2:T(2,128)S(1)} %copy.356), channel_id=8, replica_groups=mesh['expert'=8,'tensor'=4] {'expert'}, use_global_device_ids=true, to_apply=%region_50.53.clone | all-reduce | flops 8192 | bytes 65536
  1399.9 4.2 convolution_bitcast_fusion.5
  1409.6 14.9 all-reduce.18.cloned.1.call-done
  1427.7 82.3 %all-reduce.16.cloned.1.call-done = f32[985,512]{1,0:T(8,128)} async-done(((f32[985,512]{1,0:T(8,128)}), f32[985,512]{1,0:T(8,128)}) %all-reduce.16.cloned.1.call-update) | async-done | bytes 2017296 | tf_op jit(solution)/shard_map/psum | solution.py:33
  1515.9 3.7 add_add_fusion.4
  1519.6 29.1 %reduce-scatter.16.cloned.1.call-done = f32[64,4]{1,0:T(8,128)} async-done(((f32[512,4]{1,0:T(8,128)}), f32[64,4]{1,0:T(8,128)}) %reduce-scatter.16.cloned.1.call-update) | async-done | bytes 1040
  (590 shorter events, 185.9 us)
Async XLA Ops:
  7.2 140.2 %all-reduce.10.cloned.1.call-start = ((), (), s32[]{:S(2)}) async-start(), calls=%async_computation.13 | async-start | bytes 4063232 | tf_op jit(solution)/shard_map/psum | solution.py:33
  9.9 37.0 %copy-start.99 = (f32[985]{0:T(1024)}, f32[985]{0:T(1024)S(1)}, u32[]{:S(2)}) copy-start(f32[985]{0:T(1024)S(1)} %broadcast_multiply_fusion.7) | copy-start | bytes 11824
  10.3 36.5 %copy-start.127 = (f32[985]{0:T(1024)}, f32[985]{0:T(1024)S(1)}, u32[]{:S(2)}) copy-start(f32[985]{0:T(1024)S(1)} %multiply_reduce_fusion.17) | copy-start | bytes 11824
  10.3 36.5 %copy-start.118 = (f32[985]{0:T(1024)}, f32[985]{0:T(1024)S(1)}, u32[]{:S(2)}) copy-start(f32[985]{0:T(1024)S(1)} %fusion.156) | copy-start | bytes 11824
  21.3 39.8 %copy-start.65 = (bf16[2,128,512]{1,2,0:T(8,128)(2,1)}, bf16[2,128,512]{1,2,0:T(8,128)(2,1)S(1)}, u32[]{:S(2)}) copy-start(bf16[2,128,512]{1,2,0:T(8,128)(2,1)S(1)} %all_gather.26) | copy-start | bytes 786436
  46.9 103.7 %copy-start.142 = (f32[512]{0:T(512)}, f32[512]{0:T(512)S(1)}, u32[]{:S(2)}) copy-start(f32[512]{0:T(512)S(1)} %get-tuple-element.149) | copy-start | bytes 6148
  50.2 8.5 copy-start.43
  68.5 82.6 %copy-start.158 = (s32[985]{0:T(1024)}, s32[985]{0:T(1024)S(1)}, u32[]{:S(2)}) copy-start(s32[985]{0:T(1024)S(1)} %get-tuple-element.78) | copy-start | bytes 11824
  68.5 82.6 %copy-start.161 = (s32[985]{0:T(1024)}, s32[985]{0:T(1024)S(1)}, u32[]{:S(2)}) copy-start(s32[985]{0:T(1024)S(1)} %get-tuple-element.79) | copy-start | bytes 11824
  158.1 36.3 %all-to-all-start = ((bf16[8,308,512]{2,1,0:T(8,128)(2,1)}), bf16[8,308,512]{2,1,0:T(8,128)(2,1)}, u32[]{:S(2)}, u32[]{:S(2)}) async-start(bf16[8,308,512]{2,1,0:T(8,128)(2,1)} %reshape.430), calls=%async_computation | async-start | bytes 5111808 | tf_op jit(solution)/shard_map/all_to_all | solution.py:37
  162.9 138.1 %reduce-scatter.8.cloned.1.call-start = ((), (), s32[]{:S(2)}) async-start(), calls=%async_computation.14 | async-start | bytes 6389760 | tf_op jit(solution)/shard_map/reduce_scatter | solution.py:43
  165.2 33.4 %copy-start.31 = (bf16[2,1,512,512]{3,2,1,0:T(8,128)(2,1)}, bf16[2,1,512,512]{3,2,1,0:T(8,128)(2,1)S(1)}, u32[]{:S(2)}) copy-start(bf16[2,1,512,512]{3,2,1,0:T(8,128)(2,1)S(1)} %convert.8) | copy-start | bytes 3145732
  211.9 105.3 %copy-start.170 = (f32[2,512,1]{1,2,0:T(1,128)S(1)}, f32[2,512,1]{1,2,0:T(1,128)}, u32[]{:S(2)}) copy-start(f32[2,512,1]{1,2,0:T(1,128)} %param.20) | copy-start | bytes 12292
  211.9 157.9 %all-gather.5.cloned.1.call-start = ((), (), s32[]{:S(2)}) async-start(), calls=%async_computation.15 | async-start | bytes 3194880 | tf_op jit(solution)/shard_map/all_gather | solution.py:47
  302.5 23.8 %copy-start.22 = (bf16[985,512]{1,0:T(8,128)(2,1)S(1)}, bf16[985,512]{1,0:T(8,128)(2,1)}, u32[]{:S(2)}) copy-start(bf16[985,512]{1,0:T(8,128)(2,1)} %copy-done.21) | copy-start | bytes 3025924
  317.1 163.8 %all-reduce.12.cloned.1.call-start = ((), (), s32[]{:S(2)}) async-start(), calls=%async_computation.16 | async-start | bytes 4063232 | tf_op jit(solution)/shard_map/psum | solution.py:33
  347.4 27.9 %copy-start.152 = (f32[985]{0:T(1024)}, f32[985]{0:T(1024)S(1)}, u32[]{:S(2)}) copy-start(f32[985]{0:T(1024)S(1)} %get-tuple-element.76) | copy-start | bytes 11824
  347.4 27.9 %copy-start.154 = (f32[985]{0:T(1024)}, f32[985]{0:T(1024)S(1)}, u32[]{:S(2)}) copy-start(f32[985]{0:T(1024)S(1)} %get-tuple-element.77) | copy-start | bytes 11824
  347.4 25.0 %copy-start.159 = (s32[985]{0:T(1024)S(1)}, s32[985]{0:T(1024)}, u32[]{:S(2)}) copy-start(s32[985]{0:T(1024)} %copy-done.158) | copy-start | bytes 11824
  382.1 98.8 %copy-start.9 = (f32[985,512]{1,0:T(8,128)}, f32[985,512]{1,0:T(8,128)S(1)}, u32[]{:S(2)}) copy-start(f32[985,512]{1,0:T(8,128)S(1)} %get-tuple-element.102) | copy-start | bytes 6051844
  398.5 236.7 %reduce-scatter.10.cloned.1.call-start = ((), (), s32[]{:S(2)}) async-start(), calls=%async_computation.17 | async-start | bytes 6389760 | tf_op jit(solution)/shard_map/reduce_scatter | solution.py:43
  398.8 252.6 %copy-start.17 = (s32[1,985,2]{2,1,0:T(8,128)}, s32[1,985,2]{2,1,0:T(8,128)S(1)}, u32[]{:S(2)}) copy-start(s32[1,985,2]{2,1,0:T(8,128)S(1)} %copy.402) | copy-start | bytes 23644
  402.9 81.7 %copy-start.164 = (s32[985]{0:T(1024)}, s32[985]{0:T(1024)S(1)}, u32[]{:S(2)}) copy-start(s32[985]{0:T(1024)S(1)} %get-tuple-element.72) | copy-start | bytes 11824
  402.9 81.7 %copy-start.167 = (s32[985]{0:T(1024)}, s32[985]{0:T(1024)S(1)}, u32[]{:S(2)}) copy-start(s32[985]{0:T(1024)S(1)} %get-tuple-element.73) | copy-start | bytes 11824
  546.1 157.7 %all-gather.7.cloned.1.call-start = ((), (), s32[]{:S(2)}) async-start(), calls=%async_computation.18 | async-start | bytes 3194880 | tf_op jit(solution)/shard_map/all_gather | solution.py:47
  636.6 15.2 copy-start.74
  636.6 15.4 copy-start.73
  651.2 23.7 %copy-start.25 = (bf16[985,512]{1,0:T(8,128)(2,1)S(1)}, bf16[985,512]{1,0:T(8,128)(2,1)}, u32[]{:S(2)}) copy-start(bf16[985,512]{1,0:T(8,128)(2,1)} %copy-done.24) | copy-start | bytes 3025924
  651.3 254.1 %reduce-scatter.12.cloned.1.call-start = ((), (), s32[]{:S(2)}) async-start(), calls=%async_computation.19 | async-start | bytes 6389760 | tf_op jit(solution)/shard_map/reduce_scatter | solution.py:43
  663.6 44.7 %copy-start.91 = (s32[2465]{0:T(1024)}, s32[2465]{0:T(1024)S(1)}, u32[]{:S(2)}) copy-start(s32[2465]{0:T(1024)S(1)} %scatter_custom_fusion.1) | copy-start | bytes 29584
  676.1 32.3 %copy-start.168 = (s32[985]{0:T(1024)S(1)}, s32[985]{0:T(1024)}, u32[]{:S(2)}) copy-start(s32[985]{0:T(1024)} %copy-done.167) | copy-start | bytes 11824
  718.1 18.9 %copy-start.18 = (s32[1,985,2]{2,1,0:T(8,128)S(1)}, s32[1,985,2]{2,1,0:T(8,128)}, u32[]{:S(2)}) copy-start(s32[1,985,2]{2,1,0:T(8,128)} %copy-done.17) | copy-start | bytes 23644
  739.3 9.0 copy-start.123
  748.3 8.2 copy-start.156
  816.1 105.3 %copy-start.110 = (s32[985]{0:T(1024)S(1)}, s32[985]{0:T(1024)}, u32[]{:S(2)}) copy-start(s32[985]{0:T(1024)} %copy-done.108) | copy-start | bytes 11824
  816.1 105.3 %copy-start.126 = (s32[985]{0:T(1024)S(1)}, s32[985]{0:T(1024)}, u32[]{:S(2)}) copy-start(s32[985]{0:T(1024)} %copy-done.124) | copy-start | bytes 11824
  816.1 105.3 %copy-start.147 = (f32[985]{0:T(1024)S(1)}, f32[985]{0:T(1024)}, u32[]{:S(2)}) copy-start(f32[985]{0:T(1024)} %copy-done.146) | copy-start | bytes 11824
  816.1 105.3 %copy-start.149 = (f32[985]{0:T(1024)S(1)}, f32[985]{0:T(1024)}, u32[]{:S(2)}) copy-start(f32[985]{0:T(1024)} %copy-done.148) | copy-start | bytes 11824
  816.1 105.3 %copy-start.150 = (f32[985]{0:T(1024)S(1)}, f32[985]{0:T(1024)}, u32[]{:S(2)}) copy-start(f32[985]{0:T(1024)} %get-tuple-element.97) | copy-start | bytes 11824
  816.1 157.8 %all-gather.9.cloned.1.call-start = ((), (), s32[]{:S(2)}) async-start(), calls=%async_computation.20 | async-start | bytes 3194880 | tf_op jit(solution)/shard_map/all_gather | solution.py:47
  921.3 160.1 %all-reduce.14.cloned.1.call-start = ((), (), s32[]{:S(2)}) async-start(), calls=%async_computation.21 | async-start | bytes 4063232 | tf_op jit(solution)/shard_map/psum | solution.py:33
  921.4 55.3 %copy-start.166 = (s32[985]{0:T(1024)S(1)}, s32[985]{0:T(1024)}, u32[]{:S(2)}) copy-start(s32[985]{0:T(1024)} %copy-done.164) | copy-start | bytes 11824
  921.4 55.3 %copy-start.169 = (s32[985]{0:T(1024)S(1)}, s32[985]{0:T(1024)}, u32[]{:S(2)}) copy-start(s32[985]{0:T(1024)} %copy-done.167) | copy-start | bytes 11824
  996.9 84.4 %copy-start.10 = (f32[985,512]{1,0:T(8,128)S(1)}, f32[985,512]{1,0:T(8,128)}, u32[]{:S(2)}) copy-start(f32[985,512]{1,0:T(8,128)} %copy-done.9) | copy-start | bytes 6051844
  997.0 84.4 %copy-start.102 = (f32[985]{0:T(1024)S(1)}, f32[985]{0:T(1024)}, u32[]{:S(2)}) copy-start(f32[985]{0:T(1024)} %copy-done.101) | copy-start | bytes 11824
  997.0 84.4 %copy-start.121 = (f32[985]{0:T(1024)S(1)}, f32[985]{0:T(1024)}, u32[]{:S(2)}) copy-start(f32[985]{0:T(1024)} %copy-done.120) | copy-start | bytes 11824
  997.0 84.4 %copy-start.140 = (f32[512]{0:T(512)S(1)}, f32[512]{0:T(512)}, u32[]{:S(2)}) copy-start(f32[512]{0:T(512)} %get-tuple-element.83) | copy-start | bytes 6148
  999.0 84.8 %copy-start.132 = (f32[985]{0:T(1024)S(1)}, f32[985]{0:T(1024)}, u32[]{:S(2)}) copy-start(f32[985]{0:T(1024)} %copy-done.131) | copy-start | bytes 11824
  999.0 255.5 %reduce-scatter.14.cloned.1.call-start = ((), (), s32[]{:S(2)}) async-start(), calls=%async_computation.22 | async-start | bytes 6389760 | tf_op jit(solution)/shard_map/reduce_scatter | solution.py:43
  1088.9 8.7 copy-start.122
  1165.5 105.0 %copy-start.172 = (u32[32]{0:T(128)S(1)}, u32[32]{0:T(128)}, u32[]{:S(2)}) copy-start(u32[32]{0:T(128)} %constant.118) | copy-start | bytes 388
  1165.5 106.3 %copy-start.26 = (bf16[985,512]{1,0:T(8,128)(2,1)S(1)}, bf16[985,512]{1,0:T(8,128)(2,1)}, u32[]{:S(2)}) copy-start(bf16[985,512]{1,0:T(8,128)(2,1)} %copy-done.24) | copy-start | bytes 3025924
  1165.5 106.5 %copy-start.64 = (bf16[985,128]{0,1:T(8,128)(2,1)S(1)}, bf16[985,128]{0,1:T(8,128)(2,1)}, u32[]{:S(2)}) copy-start(bf16[985,128]{0,1:T(8,128)(2,1)} %copy-done.63) | copy-start | bytes 756484
  1165.5 157.5 %all-gather.11.cloned.1.call-start = ((), (), s32[]{:S(2)}) async-start(), calls=%async_computation.23 | async-start | bytes 3194880 | tf_op jit(solution)/shard_map/all_gather | solution.py:47
  1270.5 154.0 %all-reduce.18.cloned.1.call-start = ((), (), s32[]{:S(2)}) async-start(), calls=%async_computation.26 | async-start | bytes 4194304
  1275.6 52.0 %copy-start.160 = (s32[985]{0:T(1024)S(1)}, s32[985]{0:T(1024)}, u32[]{:S(2)}) copy-start(s32[985]{0:T(1024)} %copy-done.158) | copy-start | bytes 11824
  1275.6 52.0 %copy-start.163 = (s32[985]{0:T(1024)S(1)}, s32[985]{0:T(1024)}, u32[]{:S(2)}) copy-start(s32[985]{0:T(1024)} %copy-done.161) | copy-start | bytes 11824
  1350.1 8.0 copy-start.5
  1350.2 8.0 copy-start.100
  1350.2 8.0 copy-start.119
  1350.2 8.0 copy-start.138
  1364.1 145.9 %all-reduce.16.cloned.1.call-start = ((), (), s32[]{:S(2)}) async-start(), calls=%async_computation.24 | async-start | bytes 4063232 | tf_op jit(solution)/shard_map/psum | solution.py:33
  1374.0 174.7 %reduce-scatter.16.cloned.1.call-start = ((), (), s32[]{:S(2)}) async-start(), calls=%async_computation.25 | async-start | bytes 294912
  1427.7 84.8 %copy-start.128 = (f32[985]{0:T(1024)S(1)}, f32[985]{0:T(1024)}, u32[]{:S(2)}) copy-start(f32[985]{0:T(1024)} %copy-done.127) | copy-start | bytes 11824
  (124 other events, 291.4 us)
Sparse Core Ops, SparseCore 0:
  63.0 84.3 all-reduce.9
  212.0 89.0 reduce-scatter.7
  317.3 52.4 all-gather.4
  398.6 82.2 all-reduce.11
  546.2 88.8 reduce-scatter.9
  651.4 52.4 all-gather.6
  816.2 89.1 reduce-scatter.11
  921.4 52.4 all-gather.8
  999.1 82.1 all-reduce.13
  1165.6 88.8 reduce-scatter.13
  1270.6 52.4 all-gather.10
  1364.2 60.2 all-reduce.17
  1426.9 83.0 all-reduce.15
  1516.0 32.6 reduce-scatter.15
where the time goes:
time: 1570 us; the launch traced here: 1560 us
  waiting for transfers between devices  900 us (57%)
  local copies, waits for them, and re-layouts  233 us (15%)
  blocking collectives  225 us (14%)
  matrix products  122 us (8%)
  other arithmetic  53.5 us (3%)
  between operations  17.5 us (1%)
    reduce_scatter x4, waiting for transfers between devices, to_sources(): lax.psum_scatter(partial_rows, 'tensor', scatter_dimension=2, tiled=True)  356 us
    psum x4, waiting for transfers between devices, heads_total(): return lax.psum(partial_sum, 'tensor')  321 us
    all_gather x4, waiting for transfers between devices, to_sources(): return lax.all_gather(moved, 'tensor', axis=2, tiled=True)  150 us
    all_to_all x3, blocking collectives, to_experts(): lax.all_to_all(make_rows(0, model_width), 'expert', split_axis=0, concat_...  105 us
    all_to_all x4, blocking collectives, to_sources(): lax.all_to_all(shares.astype(jnp.bfloat16), 'expert', split_axis=0, conca...  58.3 us
    unnamed x16, waiting for transfers between devices  44.2 us
    gather x6, local copies, waits for them, and re-layouts, local(): gate_values = jnp.take_along_axis(probs_all, chosen, axis=1)  38.4 us
  transfers between devices with their start and end apart: 15, of which 15 were waited for; matrix products, arithmetic and copies ran while one was open for 6% of the time, Pallas kernels for 0%

commit v1 on v0

--- a/solution.py
+++ b/solution.py
@@ -30,7 +30,7 @@
 
 
 def heads_total(partial_sum):
-    return lax.psum(partial_sum, "tensor")
+    return jnp.sum(lax.all_gather(partial_sum, "tensor"), axis=0)
 
 
 def to_experts(make_rows, model_width):

time: 1570 us -> 1830 us (1.17)
  waiting for transfers between devices: 900 us -> 1130 us
  other arithmetic: 53.5 us -> 81.9 us
    all_gather x0 -> x4, waiting for transfers between devices: none -> 545 us  [heads_total(): return jnp.sum(lax.all_gather(partial_sum, 'tensor'), axis=0)]
    psum x4 -> x0, waiting for transfers between devices: 321 us -> none  [heads_total(): return lax.psum(partial_sum, 'tensor')]
    reduce_sum x0 -> x4, other arithmetic: none -> 23.3 us  [heads_total(): return jnp.sum(lax.all_gather(partial_sum, 'tensor'), axis=0)]
  transfers between devices with their start and end apart: 15 -> 15, of which waited for: 15 -> 15; matrix products, arithmetic and copies ran while one was open for 6% -> 5% of each run, Pallas kernels for 0% -> 0%
where the time goes in v1:
time: 1830 us; the launch traced here: 1820 us
  waiting for transfers between devices  1130 us (62%)
  local copies, waits for them, and re-layouts  227 us (12%)
  blocking collectives  225 us (12%)
  matrix products  134 us (7%)
  other arithmetic  81.9 us (4%)
    all_gather x4, waiting for transfers between devices, heads_total(): return jnp.sum(lax.all_gather(partial_sum, 'tensor'), axis=0)  545 us
    reduce_scatter x4, waiting for transfers between devices, to_sources(): lax.psum_scatter(partial_rows, 'tensor', scatter_dimension=2, tiled=True)  354 us
    all_gather x4, waiting for transfers between devices, to_sources(): return lax.all_gather(moved, 'tensor', axis=2, tiled=True)  164 us
    all_to_all x3, blocking collectives, to_experts(): lax.all_to_all(make_rows(0, model_width), 'expert', split_axis=0, concat_...  106 us
    all_to_all x4, blocking collectives, to_sources(): lax.all_to_all(shares.astype(jnp.bfloat16), 'expert', split_axis=0, conca...  58.2 us
    unnamed x16, waiting for transfers between devices  41.6 us
    dot_general x10, matrix products, contract_rows(): lax.dot_general(left_side, right_side, (((0,), (0,)), ((), ())), preferre...  39.4 us
    gather x6, local copies, waits for them, and re-layouts, local(): gate_values = jnp.take_along_axis(probs_all, chosen, axis=1)  38.4 us
  transfers between devices with their start and end apart: 15, of which 15 were waited for; matrix products, arithmetic and copies ran while one was open for 5% of the time, Pallas kernels for 0%

profile of v1, /device:TPU:0, one launch (start us, length us, event | category | flops | bytes accessed | tf_op | source)
XLA Modules:
  0.0 1822.7 jit_solution(2289284177472093877)
XLA Ops:
  10.5 10.8 all_gather.50
  21.3 9.3 all_gather.48
  31.0 9.4 all_gather.49
  40.4 6.6 slice_reduce_fusion.8
  81.1 126.2 %all-gather.25.cloned.1.call-done = f32[4,985,512]{2,1,0:T(8,128)} async-done(((f32[1,985,512]{2,1,0:T(8,128)}), f32[4,985,512]{2,1,0:T(8,128)}) %all-gather.25.cloned.1.call-update) | async-done | bytes 8069136 | tf_op jit(solution)/shard_map/all_gather | solution.py:33
  207.3 5.8 reduce_sum.372
  216.3 17.5 fusion.41
  233.8 4.1 reshape.430
  237.9 4.4 all-to-all-start
  246.4 27.5 %all-to-all-done = bf16[8,308,512]{2,1,0:T(8,128)(2,1)} async-done(((bf16[8,308,512]{2,1,0:T(8,128)(2,1)}), bf16[8,308,512]{2,1,0:T(8,128)(2,1)}, u32[]{:S(2)}, u32[]{:S(2)}) %all-to-all-start) | async-done | bytes 2523168 | tf_op jit(solution)/shard_map/all_to_all | solution.py:37
  273.9 4.1 reshape.431
  278.0 5.4 multiply_convert_fusion.1
  283.4 4.1 dot_general.183
  287.6 5.6 fusion.106
  293.3 88.1 %reduce-scatter.8.cloned.1.call-done = f32[8,308,128]{2,1,0:T(8,128)} async-done(((f32[8,308,512]{2,1,0:T(8,128)}), f32[8,308,128]{2,1,0:T(8,128)}) %reduce-scatter.8.cloned.1.call-update) | async-done | bytes 1261584 | tf_op jit(solution)/shard_map/reduce_scatter | solution.py:43
  382.8 14.5 all_to_all.40
  397.9 8.0 all_gather.53
  406.9 18.5 %gather_fusion = f32[1970]{0:T(1024)S(1)} fusion(f32[985,8]{0,1:T(8,128)S(1)} %fusion.142, s32[1970]{0:T(1024)S(1)} %reshape.523), kind=kCustom, calls=%fused_computation.clone | custom fusion | bytes 31520 | tf_op jit(solution)/shard_map/jit(take_along_axis)/gather | solution.py:123
  426.6 23.4 %all-gather.17.cloned.1.call-done = bf16[8,308,512]{2,1,0:T(8,128)(2,1)} async-done(((bf16[8,308,128]{2,1,0:T(8,128)(2,1)}), bf16[8,308,512]{2,1,0:T(8,128)(2,1)}) %all-gather.17.cloned.1.call-update) | async-done | bytes 2523152 | tf_op jit(solution)/shard_map/all_gather | solution.py:47
  455.6 6.7 fusion.174
  476.4 143.6 %all-gather.27.cloned.1.call-done = f32[4,985,512]{2,1,0:T(8,128)} async-done(((f32[1,985,512]{2,1,0:T(8,128)}), f32[4,985,512]{2,1,0:T(8,128)}) %all-gather.27.cloned.1.call-update) | async-done | bytes 8069136 | tf_op jit(solution)/shard_map/all_gather | solution.py:33
  620.0 5.8 reduce_sum.391
  630.3 5.5 fusion.38
  638.4 35.0 %all_to_all.41 = bf16[8,308,512]{2,1,0:T(8,128)(2,1)} all-to-all(bf16[8,308,512]{2,1,0:T(8,128)(2,1)S(1)} %reshape.434), channel_id=1, replica_groups=mesh['expert'=8,'tensor'=4] {'expert'}, dimensions={0} | all-to-all | bytes 5046272 | tf_op jit(solution)/shard_map/all_to_all | solution.py:37
  673.5 4.2 reshape.435
  677.7 5.7 multiply_convert_fusion
  686.1 4.7 fusion.104
  690.9 88.1 %reduce-scatter.10.cloned.1.call-done = f32[8,308,128]{2,1,0:T(8,128)} async-done(((f32[8,308,512]{2,1,0:T(8,128)}), f32[8,308,128]{2,1,0:T(8,128)}) %reduce-scatter.10.cloned.1.call-update) | async-done | bytes 1261584 | tf_op jit(solution)/shard_map/reduce_scatter | solution.py:43
  780.5 14.6 all_to_all.42
  796.3 10.0 scatter_custom_fusion
  807.9 39.8 %all-gather.19.cloned.1.call-done = bf16[8,308,512]{2,1,0:T(8,128)(2,1)} async-done(((bf16[8,308,128]{2,1,0:T(8,128)(2,1)}), bf16[8,308,512]{2,1,0:T(8,128)(2,1)}) %all-gather.19.cloned.1.call-update) | async-done | bytes 2523152 | tf_op jit(solution)/shard_map/all_gather | solution.py:47
  847.8 4.1 reshape.436
  851.9 4.7 fusion
  856.6 4.4 multiply_reduce_fusion.13
  861.6 18.5 %gather_fusion.1 = f32[1970]{0:T(1024)S(1)} fusion(f32[985,8]{0,1:T(8,128)S(1)} %get-tuple-element.98, s32[1970]{0:T(1024)S(1)} %reshape.528), kind=kCustom, calls=%fused_computation.2.clone | custom fusion | bytes 31520 | tf_op jit(solution)/shard_map/jit(take_along_axis)/gather | solution.py:123
  882.9 9.0 concatenate.52
  891.8 8.2 gather_fusion.2
  906.3 35.5 %all_to_all.43 = bf16[8,308,512]{2,1,0:T(8,128)(2,1)} all-to-all(bf16[8,308,512]{2,1,0:T(8,128)(2,1)S(1)} %reshape.437), channel_id=1, replica_groups=mesh['expert'=8,'tensor'=4] {'expert'}, dimensions={0} | all-to-all | bytes 5046272 | tf_op jit(solution)/shard_map/all_to_all | solution.py:37
  941.8 4.3 reshape.438
  946.1 6.5 add_convert_fusion.1
  955.2 4.8 fusion.102
  960.1 89.3 %reduce-scatter.12.cloned.1.call-done = f32[8,308,128]{2,1,0:T(8,128)} async-done(((f32[8,308,512]{2,1,0:T(8,128)}), f32[8,308,128]{2,1,0:T(8,128)}) %reduce-scatter.12.cloned.1.call-update) | async-done | bytes 1261584 | tf_op jit(solution)/shard_map/reduce_scatter | solution.py:43
  1050.8 14.5 all_to_all.44
  1065.4 52.5 %all-gather.21.cloned.1.call-done = bf16[8,308,512]{2,1,0:T(8,128)(2,1)} async-done(((bf16[8,308,128]{2,1,0:T(8,128)(2,1)}), bf16[8,308,512]{2,1,0:T(8,128)(2,1)}) %all-gather.21.cloned.1.call-update) | async-done | bytes 2523152 | tf_op jit(solution)/shard_map/all_gather | solution.py:47
  1143.3 10.0 scatter_custom_fusion.1
  1153.3 132.3 %all-gather.29.cloned.1.call-done = f32[4,985,512]{2,1,0:T(8,128)} async-done(((f32[1,985,512]{2,1,0:T(8,128)}), f32[4,985,512]{2,1,0:T(8,128)}) %all-gather.29.cloned.1.call-update) | async-done | bytes 8069136 | tf_op jit(solution)/shard_map/all_gather | solution.py:33
  1285.7 5.8 reduce_sum.413
  1299.4 8.9 concatenate.54
  1308.4 8.2 gather_fusion.3
  1322.8 35.0 %all_to_all.45 = bf16[8,308,512]{2,1,0:T(8,128)(2,1)} all-to-all(bf16[8,308,512]{2,1,0:T(8,128)(2,1)S(1)} %reshape.441), channel_id=1, replica_groups=mesh['expert'=8,'tensor'=4] {'expert'}, dimensions={0} | all-to-all | bytes 5046272 | tf_op jit(solution)/shard_map/all_to_all | solution.py:37
  1357.9 4.2 reshape.442
  1362.1 6.5 add_convert_fusion
  1371.2 4.9 fusion.100
  1376.2 88.1 %reduce-scatter.14.cloned.1.call-done = f32[8,308,128]{2,1,0:T(8,128)} async-done(((f32[8,308,512]{2,1,0:T(8,128)}), f32[8,308,128]{2,1,0:T(8,128)}) %reduce-scatter.14.cloned.1.call-update) | async-done | bytes 1261584 | tf_op jit(solution)/shard_map/reduce_scatter | solution.py:43
  1465.7 14.6 all_to_all.46
  1485.1 47.9 %all-gather.23.cloned.1.call-done = bf16[8,308,512]{2,1,0:T(8,128)(2,1)} async-done(((bf16[8,308,128]{2,1,0:T(8,128)(2,1)}), bf16[8,308,512]{2,1,0:T(8,128)(2,1)}) %all-gather.23.cloned.1.call-update) | async-done | bytes 2523152 | tf_op jit(solution)/shard_map/all_gather | solution.py:47
  1569.2 4.2 convolution_bitcast_fusion.4
  1576.2 24.2 %all-reduce.2 = f32[2,512,8]{1,0,2:T(2,128)S(1)} all-reduce(f32[2,512,8]{1,0,2:T(2,128)S(1)} %copy.356), channel_id=12, replica_groups=mesh['expert'=8,'tensor'=4] {'expert'}, use_global_device_ids=true, to_apply=%region_50.53.clone | all-reduce | flops 8192 | bytes 65536
  1601.7 4.2 convolution_bitcast_fusion.7
  1611.5 13.0 all-reduce.6.cloned.1.call-done
  1627.6 142.8 %all-gather.31.cloned.1.call-done = f32[4,985,512]{2,1,0:T(8,128)} async-done(((f32[1,985,512]{2,1,0:T(8,128)}), f32[4,985,512]{2,1,0:T(8,128)}) %all-gather.31.cloned.1.call-update) | async-done | bytes 8069136 | tf_op jit(solution)/shard_map/all_gather | solution.py:33
  1770.5 5.9 reduce_sum.428
  1782.2 3.7 add_add_fusion.4
  1785.9 28.3 %reduce-scatter.16.cloned.1.call-done = f32[64,4]{1,0:T(8,128)} async-done(((f32[512,4]{1,0:T(8,128)}), f32[64,4]{1,0:T(8,128)}) %reduce-scatter.16.cloned.1.call-update) | async-done | bytes 1040
  (578 shorter events, 198.9 us)
Async XLA Ops:
  7.2 200.2 %all-gather.25.cloned.1.call-start = ((), (), s32[]{:S(2)}) async-start(), calls=%async_computation.21 | async-start | bytes 10158080 | tf_op jit(solution)/shard_map/all_gather | solution.py:33
  9.9 37.1 %copy-start.92 = (f32[985]{0:T(1024)}, f32[985]{0:T(1024)S(1)}, u32[]{:S(2)}) copy-start(f32[985]{0:T(1024)S(1)} %broadcast_multiply_fusion.7) | copy-start | bytes 11824
  10.3 11.0 copy-start.120
  10.3 37.5 %copy-start.112 = (f32[985]{0:T(1024)}, f32[985]{0:T(1024)S(1)}, u32[]{:S(2)}) copy-start(f32[985]{0:T(1024)S(1)} %fusion.154) | copy-start | bytes 11824
  21.3 38.4 %copy-start.61 = (bf16[2,128,512]{1,2,0:T(8,128)(2,1)}, bf16[2,128,512]{1,2,0:T(8,128)(2,1)S(1)}, u32[]{:S(2)}) copy-start(bf16[2,128,512]{1,2,0:T(8,128)(2,1)S(1)} %all_gather.50) | copy-start | bytes 786436
  40.4 7.4 copy-start.35
  50.1 7.7 copy-start.39
  62.4 14.3 copy-start.17
  81.1 135.2 %copy-start.154 = (s32[985]{0:T(1024)}, s32[985]{0:T(1024)S(1)}, u32[]{:S(2)}) copy-start(s32[985]{0:T(1024)S(1)} %get-tuple-element.152) | copy-start | bytes 11824
  81.1 135.2 %copy-start.157 = (s32[985]{0:T(1024)}, s32[985]{0:T(1024)S(1)}, u32[]{:S(2)}) copy-start(s32[985]{0:T(1024)S(1)} %get-tuple-element.153) | copy-start | bytes 11824
  215.5 18.3 %copy-start.122 = (f32[985]{0:T(1024)}, f32[985]{0:T(1024)S(1)}, u32[]{:S(2)}) copy-start(f32[985]{0:T(1024)S(1)} %multiply_reduce_fusion.16) | copy-start | bytes 11824
  215.5 18.3 %copy-start.110 = (f32[985]{0:T(1024)}, f32[985]{0:T(1024)S(1)}, u32[]{:S(2)}) copy-start(f32[985]{0:T(1024)S(1)} %fusion.155) | copy-start | bytes 11824
  216.3 190.2 %copy-start.24 = (bf16[985,512]{1,0:T(8,128)(2,1)}, bf16[985,512]{1,0:T(8,128)(2,1)S(1)}, u32[]{:S(2)}) copy-start(bf16[985,512]{1,0:T(8,128)(2,1)S(1)} %multiply_convert_fusion.6) | copy-start | bytes 3025924
  237.9 36.0 %all-to-all-start = ((bf16[8,308,512]{2,1,0:T(8,128)(2,1)}), bf16[8,308,512]{2,1,0:T(8,128)(2,1)}, u32[]{:S(2)}, u32[]{:S(2)}) async-start(bf16[8,308,512]{2,1,0:T(8,128)(2,1)} %reshape.430), calls=%async_computation | async-start | bytes 5111808 | tf_op jit(solution)/shard_map/all_to_all | solution.py:37
  242.3 139.1 %reduce-scatter.8.cloned.1.call-start = ((), (), s32[]{:S(2)}) async-start(), calls=%async_computation.13 | async-start | bytes 6389760 | tf_op jit(solution)/shard_map/reduce_scatter | solution.py:43
  293.2 104.2 %copy-start.152 = (f32[2,512,1]{1,2,0:T(1,128)S(1)}, f32[2,512,1]{1,2,0:T(1,128)}, u32[]{:S(2)}) copy-start(f32[2,512,1]{1,2,0:T(1,128)} %param.20) | copy-start | bytes 12292
  293.2 156.7 %all-gather.17.cloned.1.call-start = ((), (), s32[]{:S(2)}) async-start(), calls=%async_computation.14 | async-start | bytes 3194880 | tf_op jit(solution)/shard_map/all_gather | solution.py:47
  397.3 222.7 %all-gather.27.cloned.1.call-start = ((), (), s32[]{:S(2)}) async-start(), calls=%async_computation.22 | async-start | bytes 10158080 | tf_op jit(solution)/shard_map/all_gather | solution.py:33
  406.5 19.0 %copy-start.98 = (bf16[1,512,8]{1,0,2:T(2,128)(2,1)}, bf16[1,512,8]{1,0,2:T(2,128)(2,1)S(1)}, u32[]{:S(2)}) copy-start(bf16[1,512,8]{1,0,2:T(2,128)(2,1)S(1)} %get-tuple-element.123) | copy-start | bytes 24580
  406.8 18.6 %copy-start.79 = (f32[985,8]{0,1:T(8,128)}, f32[985,8]{0,1:T(8,128)S(1)}, u32[]{:S(2)}) copy-start(f32[985,8]{0,1:T(8,128)S(1)} %get-tuple-element.133) | copy-start | bytes 94564
  406.9 18.6 %copy-start.88 = (f32[985]{0:T(1024)}, f32[985]{0:T(1024)S(1)}, u32[]{:S(2)}) copy-start(f32[985]{0:T(1024)S(1)} %get-tuple-element.132) | copy-start | bytes 11824
  406.9 18.6 %copy-start.108 = (f32[985]{0:T(1024)}, f32[985]{0:T(1024)S(1)}, u32[]{:S(2)}) copy-start(f32[985]{0:T(1024)S(1)} %fusion.143) | copy-start | bytes 11824
  426.5 29.0 %copy-start.146 = (f32[985]{0:T(1024)}, f32[985]{0:T(1024)S(1)}, u32[]{:S(2)}) copy-start(f32[985]{0:T(1024)S(1)} %get-tuple-element.76) | copy-start | bytes 11824
  426.6 29.0 %copy-start.148 = (f32[985]{0:T(1024)}, f32[985]{0:T(1024)S(1)}, u32[]{:S(2)}) copy-start(f32[985]{0:T(1024)S(1)} %get-tuple-element.77) | copy-start | bytes 11824
  426.6 26.1 %copy-start.158 = (s32[985]{0:T(1024)S(1)}, s32[985]{0:T(1024)}, u32[]{:S(2)}) copy-start(s32[985]{0:T(1024)} %copy-done.157) | copy-start | bytes 11824
  455.5 6.8 copy-start.66
  462.3 163.6 %copy-start.9 = (f32[985,512]{1,0:T(8,128)}, f32[985,512]{1,0:T(8,128)S(1)}, u32[]{:S(2)}) copy-start(f32[985,512]{1,0:T(8,128)S(1)} %get-tuple-element.102) | copy-start | bytes 6051844
  476.4 302.7 %reduce-scatter.10.cloned.1.call-start = ((), (), s32[]{:S(2)}) async-start(), calls=%async_computation.15 | async-start | bytes 6389760 | tf_op jit(solution)/shard_map/reduce_scatter | solution.py:43
  690.9 104.5 %copy-start.18 = (s32[1,985,2]{2,1,0:T(8,128)S(1)}, s32[1,985,2]{2,1,0:T(8,128)}, u32[]{:S(2)}) copy-start(s32[1,985,2]{2,1,0:T(8,128)} %copy-done.17) | copy-start | bytes 23644
  690.9 156.9 %all-gather.19.cloned.1.call-start = ((), (), s32[]{:S(2)}) async-start(), calls=%async_computation.16 | async-start | bytes 3194880 | tf_op jit(solution)/shard_map/all_gather | solution.py:47
  780.4 15.4 copy-start.75
  780.5 15.6 copy-start.74
  780.5 27.0 %copy-start.27 = (bf16[985,512]{1,0:T(8,128)(2,1)S(1)}, bf16[985,512]{1,0:T(8,128)(2,1)}, u32[]{:S(2)}) copy-start(bf16[985,512]{1,0:T(8,128)(2,1)} %copy-done.26) | copy-start | bytes 3025924
  780.5 27.0 %copy-start.100 = (bf16[1,512,8]{1,0,2:T(2,128)(2,1)S(1)}, bf16[1,512,8]{1,0,2:T(2,128)(2,1)}, u32[]{:S(2)}) copy-start(bf16[1,512,8]{1,0,2:T(2,128)(2,1)} %get-tuple-element.122) | copy-start | bytes 24580
  795.1 254.2 %reduce-scatter.12.cloned.1.call-start = ((), (), s32[]{:S(2)}) async-start(), calls=%async_computation.17 | async-start | bytes 6389760 | tf_op jit(solution)/shard_map/reduce_scatter | solution.py:43
  861.6 18.9 %copy-start.19 = (s32[1,985,2]{2,1,0:T(8,128)S(1)}, s32[1,985,2]{2,1,0:T(8,128)}, u32[]{:S(2)}) copy-start(s32[1,985,2]{2,1,0:T(8,128)} %copy-done.17) | copy-start | bytes 23644
  882.9 9.0 copy-start.116
  891.8 8.2 copy-start.150
  960.0 105.3 %copy-start.104 = (s32[985]{0:T(1024)S(1)}, s32[985]{0:T(1024)}, u32[]{:S(2)}) copy-start(s32[985]{0:T(1024)} %copy-done.102) | copy-start | bytes 11824
  960.0 105.3 %copy-start.119 = (s32[985]{0:T(1024)S(1)}, s32[985]{0:T(1024)}, u32[]{:S(2)}) copy-start(s32[985]{0:T(1024)} %copy-done.117) | copy-start | bytes 11824
  960.0 105.3 %copy-start.139 = (f32[985]{0:T(1024)S(1)}, f32[985]{0:T(1024)}, u32[]{:S(2)}) copy-start(f32[985]{0:T(1024)} %copy-done.138) | copy-start | bytes 11824
  960.0 105.3 %copy-start.141 = (f32[985]{0:T(1024)S(1)}, f32[985]{0:T(1024)}, u32[]{:S(2)}) copy-start(f32[985]{0:T(1024)} %copy-done.140) | copy-start | bytes 11824
  960.1 105.3 %copy-start.142 = (f32[985]{0:T(1024)S(1)}, f32[985]{0:T(1024)}, u32[]{:S(2)}) copy-start(f32[985]{0:T(1024)} %get-tuple-element.97) | copy-start | bytes 11824
  960.1 157.8 %all-gather.21.cloned.1.call-start = ((), (), s32[]{:S(2)}) async-start(), calls=%async_computation.18 | async-start | bytes 3194880 | tf_op jit(solution)/shard_map/all_gather | solution.py:47
  1065.3 220.4 %all-gather.29.cloned.1.call-start = ((), (), s32[]{:S(2)}) async-start(), calls=%async_computation.23 | async-start | bytes 10158080 | tf_op jit(solution)/shard_map/all_gather | solution.py:33
  1065.4 55.2 %copy-start.161 = (s32[985]{0:T(1024)S(1)}, s32[985]{0:T(1024)}, u32[]{:S(2)}) copy-start(s32[985]{0:T(1024)} %get-tuple-element.72) | copy-start | bytes 11824
  1065.4 55.2 %copy-start.163 = (s32[985]{0:T(1024)S(1)}, s32[985]{0:T(1024)}, u32[]{:S(2)}) copy-start(s32[985]{0:T(1024)} %get-tuple-element.73) | copy-start | bytes 11824
  1142.0 322.3 %reduce-scatter.14.cloned.1.call-start = ((), (), s32[]{:S(2)}) async-start(), calls=%async_computation.19 | async-start | bytes 6389760 | tf_op jit(solution)/shard_map/reduce_scatter | solution.py:43
  1153.3 138.2 %copy-start.10 = (f32[985,512]{1,0:T(8,128)S(1)}, f32[985,512]{1,0:T(8,128)}, u32[]{:S(2)}) copy-start(f32[985,512]{1,0:T(8,128)} %copy-done.9) | copy-start | bytes 6051844
  1153.3 138.2 %copy-start.95 = (f32[985]{0:T(1024)S(1)}, f32[985]{0:T(1024)}, u32[]{:S(2)}) copy-start(f32[985]{0:T(1024)} %copy-done.94) | copy-start | bytes 11824
  1153.3 138.2 %copy-start.115 = (f32[985]{0:T(1024)S(1)}, f32[985]{0:T(1024)}, u32[]{:S(2)}) copy-start(f32[985]{0:T(1024)} %copy-done.114) | copy-start | bytes 11824
  1153.3 138.2 %copy-start.133 = (f32[512]{0:T(512)S(1)}, f32[512]{0:T(512)}, u32[]{:S(2)}) copy-start(f32[512]{0:T(512)} %get-tuple-element.83) | copy-start | bytes 6148
  1376.1 104.5 %copy-start.60 = (bf16[985,128]{0,1:T(8,128)(2,1)S(1)}, bf16[985,128]{0,1:T(8,128)(2,1)}, u32[]{:S(2)}) copy-start(bf16[985,128]{0,1:T(8,128)(2,1)} %copy-done.59) | copy-start | bytes 756484
  1376.1 156.9 %all-gather.23.cloned.1.call-start = ((), (), s32[]{:S(2)}) async-start(), calls=%async_computation.20 | async-start | bytes 3194880 | tf_op jit(solution)/shard_map/all_gather | solution.py:47
  1465.7 17.5 copy-start.11
  1480.4 144.1 %all-reduce.6.cloned.1.call-start = ((), (), s32[]{:S(2)}) async-start(), calls=%async_computation.26 | async-start | bytes 4194304
  1485.1 50.6 %copy-start.156 = (s32[985]{0:T(1024)S(1)}, s32[985]{0:T(1024)}, u32[]{:S(2)}) copy-start(s32[985]{0:T(1024)} %copy-done.154) | copy-start | bytes 11824
  1485.1 50.6 %copy-start.159 = (s32[985]{0:T(1024)S(1)}, s32[985]{0:T(1024)}, u32[]{:S(2)}) copy-start(s32[985]{0:T(1024)} %copy-done.157) | copy-start | bytes 11824
  1553.1 5.2 copy-start.5
  1553.1 5.2 copy-start.93
  1553.1 5.2 copy-start.113
  1564.2 206.3 %all-gather.31.cloned.1.call-start = ((), (), s32[]{:S(2)}) async-start(), calls=%async_computation.24 | async-start | bytes 10158080 | tf_op jit(solution)/shard_map/all_gather | solution.py:33
  1567.7 246.5 %reduce-scatter.16.cloned.1.call-start = ((), (), s32[]{:S(2)}) async-start(), calls=%async_computation.25 | async-start | bytes 294912
  1601.7 5.7 copy-start.54
  (116 other events, 254.6 us)
Sparse Core Ops, SparseCore 0:
  61.6 145.6 all-gather.24
  293.3 88.0 reduce-scatter.7
  397.5 52.4 all-gather.16
  476.5 143.4 all-gather.26
  691.0 88.0 reduce-scatter.9
  795.3 52.4 all-gather.18
  960.1 89.1 reduce-scatter.11
  1065.4 52.4 all-gather.20
  1142.1 143.4 all-gather.28
  1376.3 88.0 reduce-scatter.13
  1480.5 52.4 all-gather.22
  1564.3 60.1 all-reduce.5
  1626.1 144.3 all-gather.30
  1782.3 31.8 reduce-scatter.15
